TPU v7x, 32 devices: a whole 2x2x4 slice. The times are simulated.
32 devices in a mesh: samp: 16 (over z, x, core), snp: 2 (over y).
Axes of the slice: x: 2, y: 2, z: 4, core: 2. Of those that a mesh axis runs over, the one named last changes fastest.
Arguments:
- genotypes: int32 [65536, 4096], P('samp', 'snp'), may hold values from 0 to 2, as said below
- allele_freq: float32 [4096], P('snp'), may hold values from 0.05 to 0.5
- snp_bins: int32 [4096], P('snp'), may hold values from 0 to 11, as said below
- probes: bfloat16 [64, 65536], P(None, 'samp'), may hold values from -6 to 6
- variances: float32 [13], replicated, may hold values from 0.1 to 1
Outputs:
- projected: float32 [65536, 768], P(('samp', 'snp'))
- combined: float32 [64, 65536], P(None, ('samp', 'snp'))
Inputs may be any that keep to these rules, and one draw needn't show every extreme that they name: `genotypes`: dosages 0, 1 or 2. `snp_bins`: every component has at least one SNP.
All inputs are finite; a program needn't handle non-finite values.
Results may differ from a plain program's by a relative error of at most 0.0065.
Values may be sent and summed in bfloat16 or wider, within the bound.
A program may use at most 192 MiB of HBM per device.

v0:
```python
import jax
import jax.numpy as jnp
from jax import lax
from jax.sharding import PartitionSpec as P

COMPONENTS = 12
CHUNKS = 4


def standardize(dosage_block, allele_freq):
    spread = jnp.sqrt(2.0 * allele_freq * (1.0 - allele_freq))
    return ((dosage_block.astype(jnp.float32) - 2.0 * allele_freq) / spread).astype(jnp.bfloat16)


def body(genotypes, allele_freq, snp_bins, probes, variances):
    groups = lax.axis_size("snp")
    me = lax.axis_index("snp")
    labels = jnp.arange(COMPONENTS, dtype=jnp.int32)
    onehot = (snp_bins[:, None] == labels[None, :]).astype(jnp.float32)
    counts = lax.psum(jnp.sum(onehot, 0), "snp")
    standard = standardize(genotypes, allele_freq)
    partial_scores = jnp.dot(probes, standard, preferred_element_type=jnp.float32)
    whole_rows = standard.shape[0] * lax.axis_size("samp")
    scores = lax.psum(partial_scores, "samp") / jnp.sqrt(jnp.float32(whole_rows))
    factor = jnp.sum(onehot * lax.rsqrt(counts)[None, :], 1)
    width = scores.shape[0]
    weights = (
        ((scores.T * factor[:, None])[:, None, :] * onehot[:, :, None])
        .reshape(snp_bins.shape[0], COMPONENTS * width)
        .astype(jnp.bfloat16)
    )
    own_rows = standard.shape[0] // groups
    piece = own_rows // CHUNKS

    def product(target, chunk):
        rows = lax.dynamic_slice_in_dim(standard, target * own_rows + chunk * piece, piece, 0)
        return jnp.dot(rows, weights, preferred_element_type=jnp.float32)

    got = [[] for _ in range(CHUNKS)]
    for shift in range(1, groups):
        ring = [(i, (i + shift) % groups) for i in range(groups)]
        for chunk in range(CHUNKS):
            sent = product(lax.rem(me + shift, groups), chunk).astype(jnp.bfloat16)
            got[chunk].append(lax.ppermute(sent, "snp", ring))
    blocks = []
    for chunk in range(CHUNKS):
        total = product(me, chunk)
        for term in got[chunk]:
            total = total + term.astype(jnp.float32)
        blocks.append(total)
    projected = jnp.concatenate(blocks, 0)
    stacked = projected.reshape(own_rows, COMPONENTS, width)
    own_probes = lax.dynamic_slice_in_dim(probes, me * own_rows, own_rows, 1).astype(jnp.float32)
    combined = (
        jnp.einsum("nmb,m->bn", stacked, variances[:COMPONENTS])
        + variances[COMPONENTS] * own_probes
    )
    return (projected, combined)


def solution(mesh):
    placed = (P("samp", "snp"), P("snp"), P("snp"), P(None, "samp"), P())
    return jax.shard_map(
        body,
        mesh=mesh,
        in_specs=placed,
        out_specs=(P(("samp", "snp"), None), P(None, ("samp", "snp"))),
        check_vma=False,
    )
```

profile of v0, /device:TPU:0, one launch (start us, length us, event | category | flops | bytes accessed | tf_op | source)
XLA Modules:
  0.0 278.8 jit_solution(911292419012415044)
XLA Ops:
  7.9 13.0 %divide_convert_fusion = bf16[4096,2048]{1,0:T(8,128)(2,1)S(1)} fusion(s32[4096,2048]{1,0:T(8,128)} %param.5, f32[2048]{0:T(1024)S(1)} %get-tuple-element.3, f32[2048]{0:T(1024)S(1)} %get-tuple-element.2), kind=kLoop, calls=%fused_computation | loop fusion | flops 33554432 | bytes 50348032 | tf_op jit(solution)/shard_map/convert_element_type | solution.py:12
  21.0 5.7 %copy-done = bf16[4096,2048]{1,0:T(8,128)(2,1)} copy-done((bf16[4096,2048]{1,0:T(8,128)(2,1)}, bf16[4096,2048]{1,0:T(8,128)(2,1)S(1)}, u32[]{:S(2)}) %copy-start) | copy-done | bytes 16777240
  26.7 3.9 %convolution_bitcast_fusion = f32[64,2048]{1,0:T(8,128)} fusion(bf16[64,4096]{1,0:T(8,128)(2,1)S(1)} %copy-done.2, bf16[4096,2048]{1,0:T(8,128)(2,1)S(1)} %divide_convert_fusion), kind=kOutput, calls=%fused_computation.5 | convolution fusion | flops 1073741824 | bytes 17825792 | tf_op jit(solution)/shard_map/dot_general | solution.py:22
  30.7 6.1 %psum.15 = f32[12]{0:T(128)S(1)} all-reduce(f32[12]{0:T(128)S(1)} %fusion.31), channel_id=1, replica_groups=mesh['samp'=16,'snp'=2] {'snp'}, use_global_device_ids=true, to_apply=%region_2.0 | all-reduce | flops 12 | bytes 96 | tf_op jit(solution)/shard_map/psum | solution.py:20
  37.5 86.6 %all-reduce.2.cloned.1.call-done = f32[64,2048]{1,0:T(8,128)} async-done(((f32[64,2048]{1,0:T(8,128)}), f32[64,2048]{1,0:T(8,128)}) %all-reduce.2.cloned.1.call-update) | async-done | bytes 524304 | tf_op jit(solution)/shard_map/psum | solution.py:24
  125.9 3.6 %fusion.18 = bf16[512,768]{1,0:T(8,128)(2,1)S(1)} fusion(bf16[2048,768]{0,1:T(8,128)(2,1)S(1)} %bitcast.25, bf16[4096,2048]{1,0:T(8,128)(2,1)} %copy-done, s32[]{:T(128)S(6)} %select_n.26), kind=kOutput, calls=%fused_computation.26 | convolution fusion | flops 1611005952 | bytes 6029316 | tf_op jit(solution)/shard_map/dot_general | solution.py:37
  129.5 1.5 collective-permute-start
  131.0 3.7 %fusion.21 = bf16[512,768]{1,0:T(8,128)(2,1)S(1)} fusion(bf16[2048,768]{0,1:T(8,128)(2,1)S(1)} %bitcast.26, bf16[4096,2048]{1,0:T(8,128)(2,1)} %copy-done, s32[]{:T(128)S(6)} %select_n.28), kind=kOutput, calls=%fused_computation.27 | convolution fusion | flops 1611005952 | bytes 6029316 | tf_op jit(solution)/shard_map/dot_general | solution.py:37
  134.8 1.1 collective-permute-start.1
  135.9 1.8 fusion.24
  138.7 1.8 fusion.27
  141.7 8.3 %collective-permute-done = bf16[512,768]{1,0:T(8,128)(2,1)S(1)} collective-permute-done((bf16[512,768]{1,0:T(8,128)(2,1)S(1)}, bf16[512,768]{1,0:T(8,128)(2,1)S(1)}, u32[]{:S(2)}, u32[]{:S(2)}) %collective-permute-start) | collective-permute-done | bytes 786464 | tf_op jit(solution)/shard_map/ppermute | solution.py:44
  150.0 1.8 convert_add_fusion.3
  151.8 15.0 %collective-permute-done.1 = bf16[512,768]{1,0:T(8,128)(2,1)S(1)} collective-permute-done((bf16[512,768]{1,0:T(8,128)(2,1)S(1)}, bf16[512,768]{1,0:T(8,128)(2,1)S(1)}, u32[]{:S(2)}, u32[]{:S(2)}) %collective-permute-start.1) | collective-permute-done | bytes 786464 | tf_op jit(solution)/shard_map/ppermute | solution.py:44
  166.9 1.8 convert_add_fusion.2
  168.7 15.0 %collective-permute-done.2 = bf16[512,768]{1,0:T(8,128)(2,1)S(1)} collective-permute-done((bf16[512,768]{1,0:T(8,128)(2,1)S(1)}, bf16[512,768]{1,0:T(8,128)(2,1)S(1)}, u32[]{:S(2)}, u32[]{:S(2)}) %collective-permute-start.2) | collective-permute-done | bytes 786464 | tf_op jit(solution)/shard_map/ppermute | solution.py:44
  183.7 1.8 convert_add_fusion.1
  185.5 14.4 %collective-permute-done.3 = bf16[512,768]{1,0:T(8,128)(2,1)S(1)} collective-permute-done((bf16[512,768]{1,0:T(8,128)(2,1)S(1)}, bf16[512,768]{1,0:T(8,128)(2,1)S(1)}, u32[]{:S(2)}, u32[]{:S(2)}) %collective-permute-start.3) | collective-permute-done | bytes 786464 | tf_op jit(solution)/shard_map/ppermute | solution.py:44
  200.0 2.1 convert_add_fusion
  202.0 2.9 %pad_maximum_fusion = f32[2048,768]{1,0:T(8,128)} fusion(f32[512,768]{1,0:T(8,128)S(1)} %convert_add_fusion, f32[512,768]{1,0:T(8,128)S(1)} %convert_add_fusion.1, f32[512,768]{1,0:T(8,128)S(1)} %convert_add_fusion.2, f32[512,768]{1,0:T(8,128)S(1)} %convert_add_fusion.3), kind=kLoop, calls=%fused_computation.3 | loop fusion | flops 4718592 | bytes 12582912 | tf_op jit(solution)/shard_map/concatenate | solution.py:51
  205.0 4.0 %copy.8 = bf16[2048,768]{0,1:T(8,128)(2,1)S(1)} copy(f32[2048,768]{1,0:T(8,128)} %pad_maximum_fusion) | data formatting | bytes 9437184 | tf_op jit(solution)/shard_map/concatenate | solution.py:51
  209.0 23.2 %fusion = f32[1,2048,64]{0,1,2:T(8,128)} fusion(bf16[2048,12,64]{0,2,1:T(8,128)(2,1)S(1)} %bitcast.24, f32[13]{0:T(128)S(1)} %copy-done.5), kind=kOutput, calls=%fused_computation.1 | convolution fusion | flops 3145728 | bytes 3670068 | tf_op jit(solution)/shard_map/nmb,m->bn/dot_general | solution.py:55
  232.1 38.3 %copy.10 = f32[1,2048,64]{1,2,0:T(8,128)S(1)} copy(f32[1,2048,64]{0,1,2:T(8,128)} %fusion) | data formatting | bytes 1048576 | tf_op jit(solution)/shard_map/nmb,m->bn/dot_general | solution.py:55
  270.5 1.5 bitcast_add_fusion
  (24 shorter events, 5.6 us)
Async XLA Ops:
  7.2 117.0 %all-reduce.2.cloned.1.call-start = ((), (), s32[]{:S(2)}) async-start(), calls=%async_computation | async-start | bytes 1048576 | tf_op jit(solution)/shard_map/psum | solution.py:24
  7.9 18.8 %copy-start.2 = (bf16[64,4096]{1,0:T(8,128)(2,1)S(1)}, bf16[64,4096]{1,0:T(8,128)(2,1)}, u32[]{:S(2)}) copy-start(bf16[64,4096]{1,0:T(8,128)(2,1)} %param.8) | copy-start | bytes 1572868
  20.9 5.7 %copy-start = (bf16[4096,2048]{1,0:T(8,128)(2,1)}, bf16[4096,2048]{1,0:T(8,128)(2,1)S(1)}, u32[]{:S(2)}) copy-start(bf16[4096,2048]{1,0:T(8,128)(2,1)S(1)} %divide_convert_fusion) | copy-start | bytes 50331652
  26.7 3.9 %copy-start.4 = (s32[2048]{0:T(1024)S(1)}, s32[2048]{0:T(1024)}, u32[]{:S(2)}) copy-start(s32[2048]{0:T(1024)} %param.7) | copy-start | bytes 24580
  26.7 10.3 %copy-start.5 = (f32[13]{0:T(128)S(1)}, f32[13]{0:T(128)}, u32[]{:S(2)}) copy-start(f32[13]{0:T(128)} %param.9) | copy-start | bytes 160
  125.9 9.9 %copy-start.1 = (bf16[4096,2048]{1,0:T(8,128)(2,1)S(1)}, bf16[4096,2048]{1,0:T(8,128)(2,1)}, u32[]{:S(2)}) copy-start(bf16[4096,2048]{1,0:T(8,128)(2,1)} %copy-done) | copy-start | bytes 50331652
  129.5 20.5 %collective-permute-start = (bf16[512,768]{1,0:T(8,128)(2,1)S(1)}, bf16[512,768]{1,0:T(8,128)(2,1)S(1)}, u32[]{:S(2)}, u32[]{:S(2)}) collective-permute-start(bf16[512,768]{1,0:T(8,128)(2,1)S(1)} %fusion.18), channel_id=1, source_target_pairs={{0,1},{1,0},{2,3},{3,2},{4,5},{5,4},{6,7},{7,6},{8,9},{9,8},{10,11... | collective-permute-start | bytes 2359304 | tf_op jit(solution)/shard_map/ppermute | solution.py:44
  134.8 32.1 %collective-permute-start.1 = (bf16[512,768]{1,0:T(8,128)(2,1)S(1)}, bf16[512,768]{1,0:T(8,128)(2,1)S(1)}, u32[]{:S(2)}, u32[]{:S(2)}) collective-permute-start(bf16[512,768]{1,0:T(8,128)(2,1)S(1)} %fusion.21), channel_id=1, source_target_pairs={{0,1},{1,0},{2,3},{3,2},{4,5},{5,4},{6,7},{7,6},{8,9},{9,8},{10,11... | collective-permute-start | bytes 2359304 | tf_op jit(solution)/shard_map/ppermute | solution.py:44
  137.7 46.0 %collective-permute-start.2 = (bf16[512,768]{1,0:T(8,128)(2,1)S(1)}, bf16[512,768]{1,0:T(8,128)(2,1)S(1)}, u32[]{:S(2)}, u32[]{:S(2)}) collective-permute-start(bf16[512,768]{1,0:T(8,128)(2,1)S(1)} %fusion.24), channel_id=1, source_target_pairs={{0,1},{1,0},{2,3},{3,2},{4,5},{5,4},{6,7},{7,6},{8,9},{9,8},{10,11... | collective-permute-start | bytes 2359304 | tf_op jit(solution)/shard_map/ppermute | solution.py:44
  140.6 59.4 %collective-permute-start.3 = (bf16[512,768]{1,0:T(8,128)(2,1)S(1)}, bf16[512,768]{1,0:T(8,128)(2,1)S(1)}, u32[]{:S(2)}, u32[]{:S(2)}) collective-permute-start(bf16[512,768]{1,0:T(8,128)(2,1)S(1)} %fusion.27), channel_id=1, source_target_pairs={{0,1},{1,0},{2,3},{3,2},{4,5},{5,4},{6,7},{7,6},{8,9},{9,8},{10,11... | collective-permute-start | bytes 2359304 | tf_op jit(solution)/shard_map/ppermute | solution.py:44
  232.1 38.3 %copy-start.3 = (bf16[64,4096]{1,0:T(8,128)(2,1)S(1)}, bf16[64,4096]{1,0:T(8,128)(2,1)}, u32[]{:S(2)}) copy-start(bf16[64,4096]{1,0:T(8,128)(2,1)} %param.8) | copy-start | bytes 1572868
Sparse Core Ops, SparseCore 0:
  30.7 93.4 all-reduce.1
where the time goes:
time: 280 us; the launch traced here: 279 us
  waiting for transfers between devices  139 us (50%)
  local copies, waits for them, and re-layouts  48.6 us (17%)
  matrix products  45.5 us (16%)
  other arithmetic  20.2 us (7%)
  between operations  14.2 us (5%)
  blocking collectives  6.08 us (2%)
  starting transfers between devices  4.81 us (2%)
    psum x1, waiting for transfers between devices, body(): lax.psum(partial_scores, 'samp') / jnp.sqrt(jnp.float32(whole_rows))  86.6 us
    ppermute x4, waiting for transfers between devices, body(): got[chunk].append(lax.ppermute(sent, 'snp', ring))  52.8 us
    dot_general x1, local copies, waits for them, and re-layouts, body(): jnp.einsum('nmb,m->bn', stacked, variances[:COMPONENTS])  38.3 us
    dot_general x1, matrix products, body(): jnp.einsum('nmb,m->bn', stacked, variances[:COMPONENTS])  23.2 us
    dot_general x8, matrix products, product(): return jnp.dot(rows, weights, preferred_element_type=jnp.float32)  18.4 us
    convert_element_type x1, other arithmetic, standardize(): ((dosage_block.astype(jnp.float32) - 2.0 * allele_freq) / spread).astype(...  13 us
    psum x1, blocking collectives, body(): counts = lax.psum(jnp.sum(onehot, 0), 'snp')  6.08 us
    unnamed x12, local copies, waits for them, and re-layouts  5.74 us
  transfers between devices with their start and end apart: 5, of which 5 were waited for; matrix products, arithmetic and copies ran while one was open for 5% of the time, Pallas kernels for 0%

commit v1 on v0

--- a/solution.py
+++ b/solution.py
@@ -21,7 +21,9 @@
     standard = standardize(genotypes, allele_freq)
     partial_scores = jnp.dot(probes, standard, preferred_element_type=jnp.float32)
     whole_rows = standard.shape[0] * lax.axis_size("samp")
-    scores = lax.psum(partial_scores, "samp") / jnp.sqrt(jnp.float32(whole_rows))
+    scores = jnp.sum(lax.all_gather(partial_scores, "samp"), axis=0) / jnp.sqrt(
+        jnp.float32(whole_rows)
+    )
     factor = jnp.sum(onehot * lax.rsqrt(counts)[None, :], 1)
     width = scores.shape[0]
     weights = (

time: 280 us -> 266 us (0.950)
  waiting for transfers between devices: 139 us -> 121 us
  other arithmetic: 20.2 us -> 23.1 us
    psum x1 -> x0, waiting for transfers between devices: 86.6 us -> none  [body(): lax.psum(partial_scores, 'samp') / jnp.sqrt(jnp.float32(whole_rows))]
    all_gather x0 -> x1, waiting for transfers between devices: none -> 70.2 us  [body(): lax.all_gather(partial_scores, 'samp')]
    reduce_sum x0 -> x1, other arithmetic: none -> 3.94 us  [body(): jnp.sum(lax.all_gather(partial_scores, 'samp'), axis=0)]
    unnamed x12 -> x18, local copies, waits for them, and re-layouts: 5.74 us -> 5.76 us
  transfers between devices with their start and end apart: 5 -> 5, of which waited for: 5 -> 5; matrix products, arithmetic and copies ran while one was open for 5% -> 6% of each run, Pallas kernels for 0% -> 0%
where the time goes in v1:
time: 266 us; the launch traced here: 265 us
  waiting for transfers between devices  121 us (45%)
  local copies, waits for them, and re-layouts  48.7 us (18%)
  matrix products  47.1 us (18%)
  other arithmetic  23.1 us (9%)
  between operations  14.2 us (5%)
  blocking collectives  6.08 us (2%)
  starting transfers between devices  4.6 us (2%)
    all_gather x1, waiting for transfers between devices, body(): lax.all_gather(partial_scores, 'samp')  70.2 us
    ppermute x4, waiting for transfers between devices, body(): got[chunk].append(lax.ppermute(sent, 'snp', ring))  50.9 us
    dot_general x1, local copies, waits for them, and re-layouts, body(): jnp.einsum('nmb,m->bn', stacked, variances[:COMPONENTS])  38.3 us
    dot_general x1, matrix products, body(): jnp.einsum('nmb,m->bn', stacked, variances[:COMPONENTS])  23.1 us
    dot_general x8, matrix products, product(): return jnp.dot(rows, weights, preferred_element_type=jnp.float32)  20.1 us
    convert_element_type x1, other arithmetic, standardize(): ((dosage_block.astype(jnp.float32) - 2.0 * allele_freq) / spread).astype(...  13 us
    psum x1, blocking collectives, body(): counts = lax.psum(jnp.sum(onehot, 0), 'snp')  6.08 us
    unnamed x18, local copies, waits for them, and re-layouts  5.76 us
  transfers between devices with their start and end apart: 5, of which 5 were waited for; matrix products, arithmetic and copies ran while one was open for 6% of the time, Pallas kernels for 0%

profile of v1, /device:TPU:0, one launch (start us, length us, event | category | flops | bytes accessed | tf_op | source)
XLA Modules:
  0.0 264.9 jit_solution(3947269645151700390)
XLA Ops:
  7.9 13.0 %divide_convert_fusion = bf16[4096,2048]{1,0:T(8,128)(2,1)S(1)} fusion(s32[4096,2048]{1,0:T(8,128)} %param.5, f32[2048]{0:T(1024)S(1)} %get-tuple-element.3, f32[2048]{0:T(1024)S(1)} %get-tuple-element.2), kind=kLoop, calls=%fused_computation | loop fusion | flops 33554432 | bytes 50348032 | tf_op jit(solution)/shard_map/convert_element_type | solution.py:12
  21.0 5.7 %copy-done = bf16[4096,2048]{1,0:T(8,128)(2,1)} copy-done((bf16[4096,2048]{1,0:T(8,128)(2,1)}, bf16[4096,2048]{1,0:T(8,128)(2,1)S(1)}, u32[]{:S(2)}) %copy-start) | copy-done | bytes 16777240
  26.7 3.9 %convolution_bitcast_fusion = f32[64,2048]{1,0:T(8,128)} fusion(bf16[64,4096]{1,0:T(8,128)(2,1)S(1)} %copy-done.1, bf16[4096,2048]{1,0:T(8,128)(2,1)S(1)} %divide_convert_fusion), kind=kOutput, calls=%fused_computation.5 | convolution fusion | flops 1073741824 | bytes 17825792 | tf_op jit(solution)/shard_map/dot_general | solution.py:22
  30.7 6.1 %psum.7 = f32[12]{0:T(128)S(1)} all-reduce(f32[12]{0:T(128)S(1)} %fusion.31), channel_id=1, replica_groups=mesh['samp'=16,'snp'=2] {'snp'}, use_global_device_ids=true, to_apply=%region_2.0 | all-reduce | flops 12 | bytes 96 | tf_op jit(solution)/shard_map/psum | solution.py:20
  37.5 70.2 %all-gather.3.cloned.1.call-done = f32[1024,2048]{1,0:T(8,128)} async-done(((f32[64,2048]{1,0:T(8,128)}), f32[1024,2048]{1,0:T(8,128)}) %all-gather.3.cloned.1.call-update) | async-done | bytes 8388624 | tf_op jit(solution)/shard_map/all_gather | solution.py:24
  107.7 3.9 %reduce_sum.27 = f32[64,2048]{1,0:T(8,128)S(1)} reduce(f32[16,64,2048]{2,1,0:T(8,128)} %bitcast.28, f32[]{:T(128)} %constant.31.clone.1), dimensions={0}, to_apply=%region_0.0 | reduce | flops 1966080 | bytes 8912900 | tf_op jit(solution)/shard_map/reduce_sum | solution.py:24
  112.5 3.6 %fusion.18 = bf16[512,768]{1,0:T(8,128)(2,1)S(1)} fusion(bf16[2048,768]{0,1:T(8,128)(2,1)S(1)} %bitcast.29, bf16[4096,2048]{1,0:T(8,128)(2,1)} %copy-done, s32[]{:T(128)S(6)} %select_n.26), kind=kOutput, calls=%fused_computation.26 | convolution fusion | flops 1611005952 | bytes 6029316 | tf_op jit(solution)/shard_map/dot_general | solution.py:39
  116.0 1.5 collective-permute-start
  117.6 3.4 %fusion.21 = bf16[512,768]{1,0:T(8,128)(2,1)S(1)} fusion(bf16[2048,768]{0,1:T(8,128)(2,1)S(1)} %bitcast.30, bf16[4096,2048]{1,0:T(8,128)(2,1)} %copy-done, s32[]{:T(128)S(6)} %select_n.28), kind=kOutput, calls=%fused_computation.27 | convolution fusion | flops 1611005952 | bytes 6029316 | tf_op jit(solution)/shard_map/dot_general | solution.py:39
  121.9 3.8 %fusion.24 = bf16[512,768]{1,0:T(8,128)(2,1)S(1)} fusion(bf16[2048,768]{0,1:T(8,128)(2,1)S(1)} %bitcast.31, bf16[4096,2048]{1,0:T(8,128)(2,1)} %copy-done, s32[]{:T(128)S(6)} %select_n.30), kind=kOutput, calls=%fused_computation.28 | convolution fusion | flops 1611005952 | bytes 6029316 | tf_op jit(solution)/shard_map/dot_general | solution.py:39
  126.6 1.8 fusion.27
  129.7 6.8 %collective-permute-done = bf16[512,768]{1,0:T(8,128)(2,1)S(1)} collective-permute-done((bf16[512,768]{1,0:T(8,128)(2,1)S(1)}, bf16[512,768]{1,0:T(8,128)(2,1)S(1)}, u32[]{:S(2)}, u32[]{:S(2)}) %collective-permute-start) | collective-permute-done | bytes 786464 | tf_op jit(solution)/shard_map/ppermute | solution.py:46
  136.5 1.8 convert_add_fusion.3
  138.4 15.0 %collective-permute-done.1 = bf16[512,768]{1,0:T(8,128)(2,1)S(1)} collective-permute-done((bf16[512,768]{1,0:T(8,128)(2,1)S(1)}, bf16[512,768]{1,0:T(8,128)(2,1)S(1)}, u32[]{:S(2)}, u32[]{:S(2)}) %collective-permute-start.1) | collective-permute-done | bytes 786464 | tf_op jit(solution)/shard_map/ppermute | solution.py:46
  153.4 1.8 convert_add_fusion.2
  155.2 15.0 %collective-permute-done.2 = bf16[512,768]{1,0:T(8,128)(2,1)S(1)} collective-permute-done((bf16[512,768]{1,0:T(8,128)(2,1)S(1)}, bf16[512,768]{1,0:T(8,128)(2,1)S(1)}, u32[]{:S(2)}, u32[]{:S(2)}) %collective-permute-start.2) | collective-permute-done | bytes 786464 | tf_op jit(solution)/shard_map/ppermute | solution.py:46
  170.2 2.1 convert_add_fusion.1
  172.3 14.1 %collective-permute-done.3 = bf16[512,768]{1,0:T(8,128)(2,1)S(1)} collective-permute-done((bf16[512,768]{1,0:T(8,128)(2,1)S(1)}, bf16[512,768]{1,0:T(8,128)(2,1)S(1)}, u32[]{:S(2)}, u32[]{:S(2)}) %collective-permute-start.3) | collective-permute-done | bytes 786464 | tf_op jit(solution)/shard_map/ppermute | solution.py:46
  186.4 1.8 convert_add_fusion
  188.2 2.9 %pad_maximum_fusion = f32[2048,768]{1,0:T(8,128)} fusion(f32[512,768]{1,0:T(8,128)S(1)} %convert_add_fusion, f32[512,768]{1,0:T(8,128)S(1)} %convert_add_fusion.1, f32[512,768]{1,0:T(8,128)S(1)} %convert_add_fusion.2, f32[512,768]{1,0:T(8,128)S(1)} %convert_add_fusion.3), kind=kLoop, calls=%fused_computation.3 | loop fusion | flops 4718592 | bytes 12582912 | tf_op jit(solution)/shard_map/concatenate | solution.py:53
  191.1 4.0 %copy.8 = bf16[2048,768]{0,1:T(8,128)(2,1)S(1)} copy(f32[2048,768]{1,0:T(8,128)} %pad_maximum_fusion) | data formatting | bytes 9437184 | tf_op jit(solution)/shard_map/concatenate | solution.py:53
  195.1 23.1 %fusion = f32[1,2048,64]{0,1,2:T(8,128)} fusion(bf16[2048,12,64]{0,2,1:T(8,128)(2,1)S(1)} %bitcast.27, f32[13]{0:T(128)S(1)} %copy-done.4), kind=kOutput, calls=%fused_computation.1 | convolution fusion | flops 3145728 | bytes 3670068 | tf_op jit(solution)/shard_map/nmb,m->bn/dot_general | solution.py:57
  218.3 38.3 %copy.10 = f32[1,2048,64]{1,2,0:T(8,128)S(1)} copy(f32[1,2048,64]{0,1,2:T(8,128)} %fusion) | data formatting | bytes 1048576 | tf_op jit(solution)/shard_map/nmb,m->bn/dot_general | solution.py:57
  256.6 1.5 bitcast_add_fusion
  (32 shorter events, 5.4 us)
Async XLA Ops:
  7.2 100.6 %all-gather.3.cloned.1.call-start = ((), (), s32[]{:S(2)}) async-start(), calls=%async_computation | async-start | bytes 8912896 | tf_op jit(solution)/shard_map/all_gather | solution.py:24
  7.9 18.8 %copy-start.1 = (bf16[64,4096]{1,0:T(8,128)(2,1)S(1)}, bf16[64,4096]{1,0:T(8,128)(2,1)}, u32[]{:S(2)}) copy-start(bf16[64,4096]{1,0:T(8,128)(2,1)} %param.8) | copy-start | bytes 1572868
  20.9 5.7 %copy-start = (bf16[4096,2048]{1,0:T(8,128)(2,1)}, bf16[4096,2048]{1,0:T(8,128)(2,1)S(1)}, u32[]{:S(2)}) copy-start(bf16[4096,2048]{1,0:T(8,128)(2,1)S(1)} %divide_convert_fusion) | copy-start | bytes 50331652
  26.7 3.9 %copy-start.3 = (s32[2048]{0:T(1024)S(1)}, s32[2048]{0:T(1024)}, u32[]{:S(2)}) copy-start(s32[2048]{0:T(1024)} %param.7) | copy-start | bytes 24580
  26.7 10.1 %copy-start.4 = (f32[13]{0:T(128)S(1)}, f32[13]{0:T(128)}, u32[]{:S(2)}) copy-start(f32[13]{0:T(128)} %param.9) | copy-start | bytes 160
  112.4 14.2 %slice-start = ((s8[16777216]{0:T(1024)(128)(4,1)}), s8[4194304]{0:T(1024)(128)(4,1)S(1)}, s32[]{:S(2)}) async-start(s8[16777216]{0:T(1024)(128)(4,1)} %bitcast.25), calls=%async_computation.1 | async-start | bytes 8388608
  112.4 14.2 %slice-start.1 = ((s8[16777216]{0:T(1024)(128)(4,1)}), s8[4194304]{0:T(1024)(128)(4,1)S(1)}, s32[]{:S(2)}) async-start(s8[16777216]{0:T(1024)(128)(4,1)} %bitcast.25), calls=%async_computation.2 | async-start | bytes 8388608
  116.0 10.6 %slice-start.2 = ((s8[16777216]{0:T(1024)(128)(4,1)}), s8[4194304]{0:T(1024)(128)(4,1)S(1)}, s32[]{:S(2)}) async-start(s8[16777216]{0:T(1024)(128)(4,1)} %bitcast.25), calls=%async_computation.3 | async-start | bytes 8388608
  116.0 20.5 %collective-permute-start = (bf16[512,768]{1,0:T(8,128)(2,1)S(1)}, bf16[512,768]{1,0:T(8,128)(2,1)S(1)}, u32[]{:S(2)}, u32[]{:S(2)}) collective-permute-start(bf16[512,768]{1,0:T(8,128)(2,1)S(1)} %fusion.18), channel_id=1, source_target_pairs={{0,1},{1,0},{2,3},{3,2},{4,5},{5,4},{6,7},{7,6},{8,9},{9,8},{10,11... | collective-permute-start | bytes 2359304 | tf_op jit(solution)/shard_map/ppermute | solution.py:46
  121.0 5.6 %slice-start.3 = ((s8[16777216]{0:T(1024)(128)(4,1)}), s8[4194304]{0:T(1024)(128)(4,1)S(1)}, s32[]{:S(2)}) async-start(s8[16777216]{0:T(1024)(128)(4,1)} %bitcast.25), calls=%async_computation.4 | async-start | bytes 8388608
  121.0 32.4 %collective-permute-start.1 = (bf16[512,768]{1,0:T(8,128)(2,1)S(1)}, bf16[512,768]{1,0:T(8,128)(2,1)S(1)}, u32[]{:S(2)}, u32[]{:S(2)}) collective-permute-start(bf16[512,768]{1,0:T(8,128)(2,1)S(1)} %fusion.21), channel_id=1, source_target_pairs={{0,1},{1,0},{2,3},{3,2},{4,5},{5,4},{6,7},{7,6},{8,9},{9,8},{10,11... | collective-permute-start | bytes 2359304 | tf_op jit(solution)/shard_map/ppermute | solution.py:46
  125.7 44.5 %collective-permute-start.2 = (bf16[512,768]{1,0:T(8,128)(2,1)S(1)}, bf16[512,768]{1,0:T(8,128)(2,1)S(1)}, u32[]{:S(2)}, u32[]{:S(2)}) collective-permute-start(bf16[512,768]{1,0:T(8,128)(2,1)S(1)} %fusion.24), channel_id=1, source_target_pairs={{0,1},{1,0},{2,3},{3,2},{4,5},{5,4},{6,7},{7,6},{8,9},{9,8},{10,11... | collective-permute-start | bytes 2359304 | tf_op jit(solution)/shard_map/ppermute | solution.py:46
  128.5 57.9 %collective-permute-start.3 = (bf16[512,768]{1,0:T(8,128)(2,1)S(1)}, bf16[512,768]{1,0:T(8,128)(2,1)S(1)}, u32[]{:S(2)}, u32[]{:S(2)}) collective-permute-start(bf16[512,768]{1,0:T(8,128)(2,1)S(1)} %fusion.27), channel_id=1, source_target_pairs={{0,1},{1,0},{2,3},{3,2},{4,5},{5,4},{6,7},{7,6},{8,9},{9,8},{10,11... | collective-permute-start | bytes 2359304 | tf_op jit(solution)/shard_map/ppermute | solution.py:46
  218.3 38.3 %copy-start.2 = (bf16[64,4096]{1,0:T(8,128)(2,1)S(1)}, bf16[64,4096]{1,0:T(8,128)(2,1)}, u32[]{:S(2)}) copy-start(bf16[64,4096]{1,0:T(8,128)(2,1)} %param.8) | copy-start | bytes 1572868
Sparse Core Ops, SparseCore 0:
  30.7 77.0 all-gather.2
